TPU v7x, 32 devices: a whole 2x2x4 slice. The times are simulated.
32 devices in a mesh: grp: 2 (over y), row: 4 (over z), col: 2 (over x), sub: 2 (over core).
Axes of the slice: x: 2, y: 2, z: 4, core: 2. Of those that a mesh axis runs over, the one named last changes fastest.
Arguments:
- pair: bfloat16 [96, 48, 128], P(('grp', 'row'), 'col'), parts along dimension 0, may hold values from -6 to 6
- length: int32 [2], P('grp'), parts along dimension 0, may hold values from 24 to 48
- chain: int32 [96], P('grp'), parts along dimension 0, may hold values from 0 to 3, never falling along the last dimension, each value on 1 to 24 neighbouring positions
- att_proj: bfloat16 [128, 4, 128], P(None, None, 'sub'), may hold values from -0.5 to 0.5
- att_bias: bfloat16 [128, 4], P(None, 'sub')
- chain_bias: float32 [4], P('sub'), may hold values from -2 to 2
- att_out: bfloat16 [128, 128], P('sub'), may hold values from -0.5 to 0.5
- mult_in: bfloat16 [128, 512], replicated, may hold values from -0.5 to 0.5
- mult_gate: bfloat16 [128, 128], replicated, may hold values from -0.5 to 0.5
- mult_out: bfloat16 [128, 128], replicated, may hold values from -0.5 to 0.5
- trans_up: bfloat16 [128, 512], replicated, may hold values from -0.5 to 0.5
- trans_down: bfloat16 [512, 128], replicated, may hold values from -0.25 to 0.25
Outputs:
- pair_out: bfloat16 [96, 48, 128], P(('grp', 'row'), ('col', 'sub')), parts along dimension 0
There are 2 independent parts, one for each index of `grp`. A program takes and returns all parts, laid end to end along the dimension named above; an argument that names none is the same for every part. Nothing has to cross between parts.
Inputs may be any that keep to these rules, and one draw needn't show every extreme that they name: chain numbers never fall along the residues; each chain has 1 to 24 residues.
All inputs are finite; a program needn't handle non-finite values.
Results may differ from a plain program's by a relative error of at most 0.012.
The roundings to bfloat16 on the way count: a program that leaves them out, or rounds other values in their place, can miss the bound.
Values may be sent and summed in bfloat16 or wider, within the bound.
No kernel may reach another device: no remote copies, remote signals or barrier semaphores. Data moves between devices by JAX's collectives and lax.ppermute only.
A program may use at most 64 MiB of HBM per device.

v0:
```python
import jax
import jax.numpy as jnp
from jax import lax
from jax.sharding import PartitionSpec as P


def norm(value):
    mean = jnp.mean(value, axis=-1, keepdims=True)
    centred = value - mean
    variance = jnp.mean(centred * centred, axis=-1, keepdims=True)
    return centred * lax.rsqrt(variance + 1e-05)


def local(
    pair,
    length,
    chain,
    att_proj,
    att_bias,
    chain_bias,
    att_out,
    mult_in,
    mult_gate,
    mult_out,
    trans_up,
    trans_down,
):
    rows, cols, width = pair.shape
    row_count = lax.axis_size("row")
    sub_count = lax.axis_size("sub")
    row_index = lax.axis_index("row")
    col_index = lax.axis_index("col")
    sub_index = lax.axis_index("sub")
    total = rows * row_count
    half = cols // sub_count
    heads_here = att_bias.shape[1]
    spread = att_out.shape[0]
    head_dim = spread // heads_here
    mult_width = mult_out.shape[0]
    valid = (jnp.arange(total) < length[0]).astype(jnp.float32)
    normed = norm(pair.astype(jnp.float32)).astype(jnp.bfloat16)
    flat = normed.reshape(rows * cols, width)
    projected = jnp.dot(
        flat, att_proj.reshape(width, 4 * spread), preferred_element_type=jnp.float32
    ).reshape(rows, cols, 4, spread)
    query = (projected[:, :, 0] * head_dim ** (-0.5)).astype(jnp.bfloat16)
    keys = projected[:, :, 1].astype(jnp.bfloat16)
    values = projected[:, :, 2].astype(jnp.bfloat16)
    gating = jax.nn.sigmoid(projected[:, :, 3])
    bias_local = (
        jnp.dot(flat, att_bias, preferred_element_type=jnp.float32)
        .reshape(rows, cols, heads_here)
        .transpose(2, 0, 1)
    )
    keys_all, values_all = (
        lax.all_gather(keys, "col", axis=1, tiled=True),
        lax.all_gather(values, "col", axis=1, tiled=True),
    )
    column_bias = lax.all_gather(bias_local, "row", axis=1, tiled=True)
    bias_here = lax.all_to_all(column_bias, "col", split_axis=1, concat_axis=2, tiled=True)
    chain_here = lax.dynamic_slice_in_dim(chain, col_index * cols, cols, 0)
    same = (chain_here[:, None] == chain[None, :]).astype(jnp.float32)
    bias_here = (
        bias_here
        + chain_bias[:, None, None] * same[None]
        + (valid[None, None, :] - 1.0) * 1000000000.0
    )

    def attend(block):
        block_query, block_keys, block_values = block
        scores = (
            jnp.einsum(
                "ajhd,akhd->ahjk", block_query, block_keys, preferred_element_type=jnp.float32
            )
            + bias_here[None]
        )
        weights = jax.nn.softmax(scores, axis=-1).astype(jnp.bfloat16)
        return jnp.einsum(
            "ahjk,akhd->ajhd", weights, block_values, preferred_element_type=jnp.float32
        )

    attended = lax.map(
        attend,
        (
            query.reshape(rows // 2, 2, cols, heads_here, head_dim),
            keys_all.reshape(rows // 2, 2, total, heads_here, head_dim),
            values_all.reshape(rows // 2, 2, total, heads_here, head_dim),
        ),
    )
    attended = (attended.reshape(rows, cols, spread) * gating).astype(jnp.bfloat16)
    update = jnp.dot(
        attended.reshape(rows * cols, spread), att_out, preferred_element_type=jnp.float32
    ).reshape(rows, cols, width)
    update_half = lax.psum_scatter(
        update.astype(jnp.bfloat16), "sub", scatter_dimension=1, tiled=True
    ).astype(jnp.float32)
    pair_half = lax.dynamic_slice_in_dim(pair, sub_index * half, half, 1).astype(jnp.float32)
    first = pair_half + update_half
    mixed = norm(first).astype(jnp.bfloat16)
    mixed_flat = mixed.reshape(rows * half, width)
    quad = jnp.dot(mixed_flat, mult_in, preferred_element_type=jnp.float32).reshape(
        rows, half, 4, mult_width
    )
    row_valid = lax.dynamic_slice_in_dim(valid, row_index * rows, rows, 0)
    col_valid = lax.dynamic_slice_in_dim(valid, col_index * cols + sub_index * half, half, 0)
    outer = row_valid[:, None, None] * col_valid[None, :, None]
    left = (outer * jax.nn.sigmoid(quad[:, :, 1]) * quad[:, :, 0]).astype(jnp.bfloat16)
    right = (outer * jax.nn.sigmoid(quad[:, :, 3]) * quad[:, :, 2]).astype(jnp.bfloat16)
    gate_out = jax.nn.sigmoid(jnp.dot(mixed_flat, mult_gate, preferred_element_type=jnp.float32))
    partial_value = jnp.einsum(
        "ikc,jkc->ijc",
        left,
        lax.all_gather(right, "row", axis=0, tiled=True),
        preferred_element_type=jnp.float32,
    )
    tri = lax.psum_scatter(
        partial_value.astype(jnp.bfloat16), ("col", "sub"), scatter_dimension=1, tiled=True
    ).astype(jnp.float32)
    tri_normed = norm(tri).astype(jnp.bfloat16).reshape(rows * half, mult_width)
    second = first + (
        gate_out * jnp.dot(tri_normed, mult_out, preferred_element_type=jnp.float32)
    ).reshape(rows, half, width)
    last_normed = norm(second).astype(jnp.bfloat16).reshape(rows * half, width)
    hidden = jax.nn.relu(jnp.dot(last_normed, trans_up, preferred_element_type=jnp.float32)).astype(
        jnp.bfloat16
    )
    result = second + jnp.dot(hidden, trans_down, preferred_element_type=jnp.float32).reshape(
        rows, half, width
    )
    return result.astype(jnp.bfloat16)


def solution(mesh):
    placed = (
        P(("grp", "row"), "col", None),
        P("grp"),
        P("grp"),
        P(None, None, "sub"),
        P(None, "sub"),
        P("sub"),
        P("sub", None),
        P(),
        P(),
        P(),
        P(),
        P(),
    )
    return jax.shard_map(
        local,
        mesh=mesh,
        in_specs=placed,
        out_specs=P(("grp", "row"), ("col", "sub"), None),
        check_vma=False,
    )
```

profile of v0, /device:TPU:0, one launch (start us, length us, event | category | flops | bytes accessed | tf_op | source)
XLA Modules:
  0.0 124.0 jit_solution(8940343694213639194)
XLA Ops:
  6.5 1.0 convert_reduce_fusion
  7.6 1.1 fusion.21
  8.7 1.2 convolution_bitcast_fusion.1
  9.9 14.8 %all_gather.14 = f32[2,48,24]{2,0,1:T(2,128)S(1)} all-gather(f32[2,12,24]{2,0,1:T(2,128)S(1)} %convolution_bitcast_fusion.1), channel_id=1, replica_groups=mesh['grp'=2,'row'=4,'col'=2,'sub'=2] {'row'}, dimensions={1}, use_global_device_ids=true | all-gather | bytes 11520 | tf_op jit(solution)/shard_map/all_gather | solution.py:59
  24.6 0.7 reshape.214
  25.4 3.2 %all-to-all-start = ((f32[2,1,1152]{2,1,0:T(1,128)}), f32[2,1,1152]{2,1,0:T(1,128)S(1)}, u32[]{:S(2)}, u32[]{:S(2)}) async-start(f32[2,1,1152]{2,1,0:T(1,128)} %reshape.214), calls=%async_computation | async-start | bytes 18432 | tf_op jit(solution)/shard_map/all_to_all | solution.py:60
  28.7 0.7 dynamic_slice.24
  29.4 0.7 compare_convert_fusion
  30.8 1.2 fusion.72
  32.0 5.4 %all-gather = bf16[12,48,1,64]{3,1,2,0:T(8,128)(2,1)S(1)} all-gather(bf16[12,24,1,64]{3,1,2,0:T(8,128)(2,1)S(1)} %get-tuple-element.85), channel_id=2, replica_groups=mesh['grp'=2,'row'=4,'col'=2,'sub'=2] {'col'}, dimensions={1}, use_global_device_ids=true | all-gather | bytes 110592 | tf_op jit(solution)/shard_map/all_gather | solution.py:57
  37.6 5.2 %all-gather.1 = bf16[12,48,1,64]{3,1,2,0:T(8,128)(2,1)S(1)} all-gather(bf16[12,24,1,64]{3,1,2,0:T(8,128)(2,1)S(1)} %get-tuple-element.84), channel_id=3, replica_groups=mesh['grp'=2,'row'=4,'col'=2,'sub'=2] {'col'}, dimensions={1}, use_global_device_ids=true | all-gather | bytes 110592 | tf_op jit(solution)/shard_map/all_gather | solution.py:56
  43.2 0.5 broadcast.191
  43.7 0.7 reduce
  44.8 4.9 %while.10 = (s32[]{:T(128)}, f32[6,2,24,2,32]{4,3,2,1,0:T(2,128)S(1)}, bf16[6,2,48,2,32]{2,4,3,1,0:T(8,128)(2,1)S(1)}, bf16[6,2,24,2,32]{4,3,2,1,0:T(2,128)(2,1)...) while((s32[]{:T(128)}, f32[6,2,24,2,32]{4,3,2,1,0:T(2,128)S(1)}, ...), condition=%wide.region_5.6_spmd, body=%wide.region_2.5_spmd.sunk | while | flops 917184 | bytes 438753 | solution.py:82
  47.4 0.3 fusion.93
  48.2 0.3 fusion.93
  49.9 0.8 convolution_convert_fusion.1
  51.0 0.6 dynamic-slice
  52.2 17.7 %all-reduce.3.cloned.1.call-done = bf16[12,24,128]{2,1,0:T(8,128)(2,1)} async-done(((bf16[12,24,128]{2,1,0:T(8,128)(2,1)}), bf16[12,24,128]{2,1,0:T(8,128)(2,1)}) %all-reduce.3.cloned.1.call-update) | async-done | bytes 73744
  69.9 1.0 fusion.52
  71.0 1.1 multiply_reduce_fusion.1
  72.1 1.0 multiply_convert_fusion.1
  73.4 14.1 %all_gather.15 = bf16[48,12,128]{2,1,0:T(8,128)(2,1)S(1)} all-gather(bf16[12,12,128]{2,1,0:T(8,128)(2,1)S(1)} %get-tuple-element.83), channel_id=1, replica_groups=mesh['grp'=2,'row'=4,'col'=2,'sub'=2] {'row'}, dimensions={0}, use_global_device_ids=true | all-gather | bytes 184320 | tf_op jit(solution)/shard_map/all_gather | solution.py:113
  87.5 1.0 copy.77
  88.5 0.5 copy.78
  89.0 0.9 fusion.13
  89.9 1.2 copy.79
  91.4 20.9 %reduce-scatter.3.cloned.1.call-done = bf16[12,12,128]{2,0,1:T(8,128)(2,1)} async-done(((bf16[12,48,128]{2,0,1:T(8,128)(2,1)}), bf16[12,12,128]{2,0,1:T(8,128)(2,1)}) %reduce-scatter.3.cloned.1.call-update) | async-done | bytes 36880 | tf_op jit(solution)/shard_map/reduce_scatter | solution.py:116
  112.3 0.9 convert_reduce_fusion.1
  113.4 1.0 fusion.33
  114.6 0.9 fusion.34
  116.6 0.6 add_convert_fusion
  (95 shorter events, 7.4 us)
Async XLA Ops:
  6.5 109.7 %copy-start = (bf16[512,128]{1,0:T(8,128)(2,1)S(1)}, bf16[512,128]{1,0:T(8,128)(2,1)}, u32[]{:S(2)}) copy-start(bf16[512,128]{1,0:T(8,128)(2,1)} %param.25) | copy-start | bytes 393220
  25.4 17.8 %all-to-all-start = ((f32[2,1,1152]{2,1,0:T(1,128)}), f32[2,1,1152]{2,1,0:T(1,128)S(1)}, u32[]{:S(2)}, u32[]{:S(2)}) async-start(f32[2,1,1152]{2,1,0:T(1,128)} %reshape.214), calls=%async_computation | async-start | bytes 18432 | tf_op jit(solution)/shard_map/all_to_all | solution.py:60
  28.6 41.3 %all-reduce.3.cloned.1.call-start = ((), (), s32[]{:S(2)}) async-start(), calls=%async_computation.3 | async-start | bytes 147456
  30.8 13.9 %copy-start.6 = (f32[2]{0:T(128)S(1)}, f32[2]{0:T(128)}, u32[]{:S(2)}) copy-start(f32[2]{0:T(128)} %param.19) | copy-start | bytes 28
  44.8 5.1 %copy-start.8 = (bf16[64,128]{1,0:T(8,128)(2,1)S(1)}, bf16[64,128]{1,0:T(8,128)(2,1)}, u32[]{:S(2)}) copy-start(bf16[64,128]{1,0:T(8,128)(2,1)} %param.20) | copy-start | bytes 49156
  44.8 6.1 %copy-start.4 = (bf16[128,512]{1,0:T(8,128)(2,1)S(1)}, bf16[128,512]{1,0:T(8,128)(2,1)}, u32[]{:S(2)}) copy-start(bf16[128,512]{1,0:T(8,128)(2,1)} %param.21) | copy-start | bytes 393220
  44.8 6.2 %copy-start.9 = (u32[32]{0:T(128)S(1)}, u32[32]{0:T(128)}, u32[]{:S(2)}) copy-start(u32[32]{0:T(128)} %constant.70) | copy-start | bytes 388
  49.7 20.3 %copy-start.1 = (bf16[12,24,128]{2,1,0:T(8,128)(2,1)S(1)}, bf16[12,24,128]{2,1,0:T(8,128)(2,1)}, u32[]{:S(2)}) copy-start(bf16[12,24,128]{2,1,0:T(8,128)(2,1)} %param.14) | copy-start | bytes 221188
  50.7 61.6 %reduce-scatter.3.cloned.1.call-start = ((), (), s32[]{:S(2)}) async-start(), calls=%async_computation.2 | async-start | bytes 245760 | tf_op jit(solution)/shard_map/reduce_scatter | solution.py:116
  89.0 2.2 %copy-start.7 = (bf16[128,128]{1,0:T(8,128)(2,1)S(1)}, bf16[128,128]{1,0:T(8,128)(2,1)}, u32[]{:S(2)}) copy-start(bf16[128,128]{1,0:T(8,128)(2,1)} %param.22) | copy-start | bytes 98308
  89.9 25.7 %copy-start.5 = (bf16[128,128]{1,0:T(8,128)(2,1)S(1)}, bf16[128,128]{1,0:T(8,128)(2,1)}, u32[]{:S(2)}) copy-start(bf16[128,128]{1,0:T(8,128)(2,1)} %param.23) | copy-start | bytes 98308
  89.9 25.8 %copy-start.2 = (bf16[12,24,128]{2,1,0:T(8,128)(2,1)S(1)}, bf16[12,24,128]{2,1,0:T(8,128)(2,1)}, u32[]{:S(2)}) copy-start(bf16[12,24,128]{2,1,0:T(8,128)(2,1)} %all-reduce.3.cloned.1.call-done) | copy-start | bytes 221188
  89.9 26.3 %copy-start.3 = (bf16[128,512]{1,0:T(8,128)(2,1)S(1)}, bf16[128,512]{1,0:T(8,128)(2,1)}, u32[]{:S(2)}) copy-start(bf16[128,512]{1,0:T(8,128)(2,1)} %param.24) | copy-start | bytes 393220
Sparse Core Ops, SparseCore 0:
  50.8 19.0 all-reduce.2
  91.3 20.9 reduce-scatter.2
where the time goes:
time: 125 us; the launch traced here: 124 us
  blocking collectives  39.5 us (32%)
  waiting for transfers between devices  38.7 us (31%)
  between operations  15.2 us (12%)
  other arithmetic  10.7 us (9%)
  matrix products  9.25 us (7%)
  local copies, waits for them, and re-layouts  7.19 us (6%)
  starting transfers between devices  3.31 us (3%)
    reduce_scatter x1, waiting for transfers between devices, local(): lax.psum_scatter(partial_value.astype(jnp.bfloat16), ('col', 'sub'), scat...  20.9 us
    unnamed x3, waiting for transfers between devices  17.8 us
    all_gather x1, blocking collectives, local(): column_bias = lax.all_gather(bias_local, 'row', axis=1, tiled=True)  14.8 us
    all_gather x1, blocking collectives, local(): lax.all_gather(right, 'row', axis=0, tiled=True)  14.1 us
    all_gather x1, blocking collectives, local(): lax.all_gather(values, 'col', axis=1, tiled=True)  5.44 us
    all_gather x1, blocking collectives, local(): lax.all_gather(keys, 'col', axis=1, tiled=True)  5.2 us
    reduce_sum x4, other arithmetic, norm(): variance = jnp.mean(centred * centred, axis=-1, keepdims=True)  3.31 us
    all_to_all x1, starting transfers between devices, local(): lax.all_to_all(column_bias, 'col', split_axis=1, concat_axis=2, tiled=True)  3.23 us
  transfers between devices with their start and end apart: 3, of which 2 were waited for; matrix products, arithmetic and copies ran while one was open for 3% of the time, Pallas kernels for 0%

commit v1 on v0

--- a/solution.py
+++ b/solution.py
@@ -56,7 +56,14 @@
         lax.all_gather(keys, "col", axis=1, tiled=True),
         lax.all_gather(values, "col", axis=1, tiled=True),
     )
-    column_bias = lax.all_gather(bias_local, "row", axis=1, tiled=True)
+    count = lax.axis_size("row")
+    route = [(i, (i + 1) % count) for i in range(count)]
+    parts = [bias_local]
+    for reach in range(1, count):
+        parts = [lax.ppermute(parts[0], "row", route), *parts]
+    out = jnp.concatenate(parts, axis=1)
+    shift = (lax.axis_index("row") + 1) * parts[-1].shape[1]
+    column_bias = jnp.roll(out, shift, axis=1)
     bias_here = lax.all_to_all(column_bias, "col", split_axis=1, concat_axis=2, tiled=True)
     chain_here = lax.dynamic_slice_in_dim(chain, col_index * cols, cols, 0)
     same = (chain_here[:, None] == chain[None, :]).astype(jnp.float32)

time: 125 us -> 119 us (0.952)
  blocking collectives: 39.5 us -> 24.1 us
  waiting for transfers between devices: 38.7 us -> 43.9 us
  starting transfers between devices: 3.31 us -> 7.72 us
    all_gather x1 -> x0, blocking collectives: 14.8 us -> none  [local(): column_bias = lax.all_gather(bias_local, 'row', axis=1, tiled=True)]
    ppermute x0 -> x3, waiting for transfers between devices: none -> 4.87 us  [local(): parts = [lax.ppermute(parts[0], 'row', route), *parts]]
    ppermute x0 -> x3, starting transfers between devices: none -> 4.41 us  [local(): parts = [lax.ppermute(parts[0], 'row', route), *parts]]
  transfers between devices with their start and end apart: 3 -> 6, of which waited for: 2 -> 5; matrix products, arithmetic and copies ran while one was open for 3% -> 3% of each run, Pallas kernels for 0% -> 0%
where the time goes in v1:
time: 119 us; the launch traced here: 118 us
  waiting for transfers between devices  43.9 us (37%)
  blocking collectives  24.1 us (20%)
  between operations  15.2 us (13%)
  other arithmetic  10.7 us (9%)
  matrix products  9.26 us (8%)
  starting transfers between devices  7.72 us (6%)
  local copies, waits for them, and re-layouts  7.26 us (6%)
    reduce_scatter x1, waiting for transfers between devices, local(): lax.psum_scatter(partial_value.astype(jnp.bfloat16), ('col', 'sub'), scat...  21 us
    unnamed x3, waiting for transfers between devices  18.1 us
    all_gather x1, blocking collectives, local(): lax.all_gather(right, 'row', axis=0, tiled=True)  14.1 us
    all_gather x1, blocking collectives, local(): lax.all_gather(keys, 'col', axis=1, tiled=True)  5.02 us
    all_gather x1, blocking collectives, local(): lax.all_gather(values, 'col', axis=1, tiled=True)  5.01 us
    ppermute x3, waiting for transfers between devices, local(): parts = [lax.ppermute(parts[0], 'row', route), *parts]  4.87 us
    ppermute x3, starting transfers between devices, local(): parts = [lax.ppermute(parts[0], 'row', route), *parts]  4.41 us
    reduce_sum x4, other arithmetic, norm(): variance = jnp.mean(centred * centred, axis=-1, keepdims=True)  3.31 us
  transfers between devices with their start and end apart: 6, of which 5 were waited for; matrix products, arithmetic and copies ran while one was open for 3% of the time, Pallas kernels for 0%

profile of v1, /device:TPU:0, one launch (start us, length us, event | category | flops | bytes accessed | tf_op | source)
XLA Modules:
  0.0 118.4 jit_solution(5342397341412451744)
XLA Ops:
  6.5 1.0 convert_reduce_fusion
  7.6 1.1 fusion.21
  8.7 1.2 %convolution_bitcast_fusion.1 = f32[2,12,24]{2,0,1:T(2,128)S(1)} fusion(bf16[12,24,128]{2,1,0:T(8,128)(2,1)} %param.14, f32[12,24]{1,0:T(8,128)S(1)} %add_rsqrt_fusion.3, f32[12,24]{1,0:T(8,128)S(1)} %broadcast_multiply_fusion.4, bf16[128,2]{0,1:T(2,128)(2,1)} %param.18), kind=kOutput, calls=%fused_computation.28 | convolution fusion | flops 294912 | bytes 78848 | tf_op jit(solution)/shard_map/dot_general | solution.py:51
  9.9 3.1 %collective-permute-start = (f32[2,12,24]{2,0,1:T(2,128)S(1)}, f32[2,12,24]{2,0,1:T(2,128)S(1)}, u32[]{:S(2)}, u32[]{:S(2)}) collective-permute-start(f32[2,12,24]{2,0,1:T(2,128)S(1)} %convolution_bitcast_fusion.1), channel_id=1, source_target_pairs={{0,4},{4,8},{8,12},{12,0},{1,5},{5,9},{9,13},{13,1},{2,6},{6,10},{... | collective-permute-start | bytes 6920 | tf_op jit(solution)/shard_map/ppermute | solution.py:63
  12.9 0.7 dynamic_slice.29
  13.7 0.7 compare_convert_fusion
  15.1 1.2 %fusion.72 = (bf16[12,24,4,64]{3,1,2,0:T(8,128)(2,1)S(1)}, f32[12,24,4,64]{3,1,2,0:T(8,128)S(1)}) fusion(bf16[128,4,64]{0,2,1:T(8,128)(2,1)} %param.17, f32[12,24]{1,0:T(8,128)S(1)} %add_rsqrt_fusion.3, f32[12,24]{1,0:T(8,128)S(1)} %broadcast_multiply_fusion.4, bf16[12,24,128]{2,1,0:T(8,128)(2,1)} %param.14), kind=kOutput, calls=%fused_computation.114 | convolution fusion | flops 19095552 | bytes 583936 | tf_op jit(solution)/shard_map/dot_general | solution.py:43
  16.6 1.3 %collective-permute-start.1 = (f32[2,12,24]{2,0,1:T(2,128)S(1)}, f32[2,12,24]{2,0,1:T(2,128)S(1)}, u32[]{:S(2)}, u32[]{:S(2)}) collective-permute-start(f32[2,12,24]{2,0,1:T(2,128)S(1)} %collective-permute-done), channel_id=1, source_target_pairs={{0,4},{4,8},{8,12},{12,0},{1,5},{5,9},{9,13},{13,1},{2,6},{6,10},{... | collective-permute-start | bytes 6920 | tf_op jit(solution)/shard_map/ppermute | solution.py:63
  18.0 4.1 %collective-permute-done.1 = f32[2,12,24]{2,0,1:T(2,128)S(1)} collective-permute-done((f32[2,12,24]{2,0,1:T(2,128)S(1)}, f32[2,12,24]{2,0,1:T(2,128)S(1)}, u32[]{:S(2)}, u32[]{:S(2)}) %collective-permute-start.1) | collective-permute-done | bytes 2336 | tf_op jit(solution)/shard_map/ppermute | solution.py:63
  22.1 5.0 %all-gather = bf16[12,48,1,64]{3,1,2,0:T(8,128)(2,1)S(1)} all-gather(bf16[12,24,1,64]{3,1,2,0:T(8,128)(2,1)S(1)} %get-tuple-element.91), channel_id=2, replica_groups=mesh['grp'=2,'row'=4,'col'=2,'sub'=2] {'col'}, dimensions={1}, use_global_device_ids=true | all-gather | bytes 110592 | tf_op jit(solution)/shard_map/all_gather | solution.py:57
  27.1 0.5 collective-permute-done.2
  27.7 0.7 reshape.214
  28.5 3.2 %all-to-all-start = ((f32[2,1,1152]{2,1,0:T(1,128)}), f32[2,1,1152]{2,1,0:T(1,128)S(1)}, u32[]{:S(2)}, u32[]{:S(2)}) async-start(f32[2,1,1152]{2,1,0:T(1,128)} %reshape.214), calls=%async_computation | async-start | bytes 18432 | tf_op jit(solution)/shard_map/all_to_all | solution.py:67
  31.7 5.0 %all-gather.1 = bf16[12,48,1,64]{3,1,2,0:T(8,128)(2,1)S(1)} all-gather(bf16[12,24,1,64]{3,1,2,0:T(8,128)(2,1)S(1)} %get-tuple-element.90), channel_id=3, replica_groups=mesh['grp'=2,'row'=4,'col'=2,'sub'=2] {'col'}, dimensions={1}, use_global_device_ids=true | all-gather | bytes 110592 | tf_op jit(solution)/shard_map/all_gather | solution.py:56
  37.2 0.5 broadcast.191
  37.7 0.7 reduce
  38.8 4.9 %while.10 = (s32[]{:T(128)}, f32[6,2,24,2,32]{4,3,2,1,0:T(2,128)S(1)}, bf16[6,2,48,2,32]{2,4,3,1,0:T(8,128)(2,1)S(1)}, bf16[6,2,24,2,32]{4,3,2,1,0:T(2,128)(2,1)...) while((s32[]{:T(128)}, f32[6,2,24,2,32]{4,3,2,1,0:T(2,128)S(1)}, ...), condition=%wide.region_5.6_spmd, body=%wide.region_2.5_spmd.sunk | while | flops 917184 | bytes 438753 | solution.py:89
  43.9 0.8 convolution_convert_fusion.1
  45.0 0.6 dynamic-slice
  46.2 18.0 %all-reduce.3.cloned.1.call-done = bf16[12,24,128]{2,1,0:T(8,128)(2,1)} async-done(((bf16[12,24,128]{2,1,0:T(8,128)(2,1)}), bf16[12,24,128]{2,1,0:T(8,128)(2,1)}) %all-reduce.3.cloned.1.call-update) | async-done | bytes 73744
  64.2 1.0 fusion.52
  65.2 1.1 multiply_reduce_fusion.1
  66.3 1.0 multiply_convert_fusion.1
  67.7 14.1 %all_gather.11 = bf16[48,12,128]{2,1,0:T(8,128)(2,1)S(1)} all-gather(bf16[12,12,128]{2,1,0:T(8,128)(2,1)S(1)} %get-tuple-element.89), channel_id=1, replica_groups=mesh['grp'=2,'row'=4,'col'=2,'sub'=2] {'row'}, dimensions={0}, use_global_device_ids=true | all-gather | bytes 184320 | tf_op jit(solution)/shard_map/all_gather | solution.py:120
  81.8 1.0 copy.120
  83.3 0.9 fusion.13
  84.2 1.2 %copy.122 = bf16[12,48,128]{2,0,1:T(8,128)(2,1)} copy(bf16[12,48,128]{1,0,2:T(8,128)(2,1)S(1)} %fusion.13) | data formatting | bytes 294912 | tf_op jit(solution)/shard_map/convert_element_type | solution.py:124
  85.6 21.0 %reduce-scatter.3.cloned.1.call-done = bf16[12,12,128]{2,0,1:T(8,128)(2,1)} async-done(((bf16[12,48,128]{2,0,1:T(8,128)(2,1)}), bf16[12,12,128]{2,0,1:T(8,128)(2,1)}) %reduce-scatter.3.cloned.1.call-update) | async-done | bytes 36880 | tf_op jit(solution)/shard_map/reduce_scatter | solution.py:123
  106.6 0.9 convert_reduce_fusion.1
  107.7 1.0 fusion.33
  108.9 0.9 fusion.34
  110.9 0.6 add_convert_fusion
  (109 shorter events, 8.7 us)
Async XLA Ops:
  6.5 104.0 %copy-start = (bf16[512,128]{1,0:T(8,128)(2,1)S(1)}, bf16[512,128]{1,0:T(8,128)(2,1)}, u32[]{:S(2)}) copy-start(bf16[512,128]{1,0:T(8,128)(2,1)} %param.25) | copy-start | bytes 393220
  9.9 6.8 %collective-permute-start = (f32[2,12,24]{2,0,1:T(2,128)S(1)}, f32[2,12,24]{2,0,1:T(2,128)S(1)}, u32[]{:S(2)}, u32[]{:S(2)}) collective-permute-start(f32[2,12,24]{2,0,1:T(2,128)S(1)} %convolution_bitcast_fusion.1), channel_id=1, source_target_pairs={{0,4},{4,8},{8,12},{12,0},{1,5},{5,9},{9,13},{13,1},{2,6},{6,10},{... | collective-permute-start | bytes 6920 | tf_op jit(solution)/shard_map/ppermute | solution.py:63
  15.0 23.6 %copy-start.6 = (f32[2]{0:T(128)S(1)}, f32[2]{0:T(128)}, u32[]{:S(2)}) copy-start(f32[2]{0:T(128)} %param.19) | copy-start | bytes 28
  16.6 5.5 %collective-permute-start.1 = (f32[2,12,24]{2,0,1:T(2,128)S(1)}, f32[2,12,24]{2,0,1:T(2,128)S(1)}, u32[]{:S(2)}, u32[]{:S(2)}) collective-permute-start(f32[2,12,24]{2,0,1:T(2,128)S(1)} %collective-permute-done), channel_id=1, source_target_pairs={{0,4},{4,8},{8,12},{12,0},{1,5},{5,9},{9,13},{13,1},{2,6},{6,10},{... | collective-permute-start | bytes 6920 | tf_op jit(solution)/shard_map/ppermute | solution.py:63
  22.1 5.5 %collective-permute-start.2 = (f32[2,12,24]{2,0,1:T(2,128)S(1)}, f32[2,12,24]{2,0,1:T(2,128)S(1)}, u32[]{:S(2)}, u32[]{:S(2)}) collective-permute-start(f32[2,12,24]{2,0,1:T(2,128)S(1)} %collective-permute-done.1), channel_id=1, source_target_pairs={{0,4},{4,8},{8,12},{12,0},{1,5},{5,9},{9,13},{13,1},{2,6},{6,10},{... | collective-permute-start | bytes 6920 | tf_op jit(solution)/shard_map/ppermute | solution.py:63
  28.5 8.7 %all-to-all-start = ((f32[2,1,1152]{2,1,0:T(1,128)}), f32[2,1,1152]{2,1,0:T(1,128)S(1)}, u32[]{:S(2)}, u32[]{:S(2)}) async-start(f32[2,1,1152]{2,1,0:T(1,128)} %reshape.214), calls=%async_computation | async-start | bytes 18432 | tf_op jit(solution)/shard_map/all_to_all | solution.py:67
  31.7 32.5 %all-reduce.3.cloned.1.call-start = ((), (), s32[]{:S(2)}) async-start(), calls=%async_computation.3 | async-start | bytes 147456
  38.7 5.1 %copy-start.8 = (bf16[64,128]{1,0:T(8,128)(2,1)S(1)}, bf16[64,128]{1,0:T(8,128)(2,1)}, u32[]{:S(2)}) copy-start(bf16[64,128]{1,0:T(8,128)(2,1)} %param.20) | copy-start | bytes 49156
  38.8 6.1 %copy-start.4 = (bf16[128,512]{1,0:T(8,128)(2,1)S(1)}, bf16[128,512]{1,0:T(8,128)(2,1)}, u32[]{:S(2)}) copy-start(bf16[128,512]{1,0:T(8,128)(2,1)} %param.21) | copy-start | bytes 393220
  38.8 6.2 %copy-start.9 = (u32[32]{0:T(128)S(1)}, u32[32]{0:T(128)}, u32[]{:S(2)}) copy-start(u32[32]{0:T(128)} %constant.89) | copy-start | bytes 388
  43.7 20.6 %copy-start.1 = (bf16[12,24,128]{2,1,0:T(8,128)(2,1)S(1)}, bf16[12,24,128]{2,1,0:T(8,128)(2,1)}, u32[]{:S(2)}) copy-start(bf16[12,24,128]{2,1,0:T(8,128)(2,1)} %param.14) | copy-start | bytes 221188
  44.7 61.9 %reduce-scatter.3.cloned.1.call-start = ((), (), s32[]{:S(2)}) async-start(), calls=%async_computation.2 | async-start | bytes 245760 | tf_op jit(solution)/shard_map/reduce_scatter | solution.py:123
  83.2 2.2 %copy-start.7 = (bf16[128,128]{1,0:T(8,128)(2,1)S(1)}, bf16[128,128]{1,0:T(8,128)(2,1)}, u32[]{:S(2)}) copy-start(bf16[128,128]{1,0:T(8,128)(2,1)} %param.22) | copy-start | bytes 98308
  84.2 25.7 %copy-start.5 = (bf16[128,128]{1,0:T(8,128)(2,1)S(1)}, bf16[128,128]{1,0:T(8,128)(2,1)}, u32[]{:S(2)}) copy-start(bf16[128,128]{1,0:T(8,128)(2,1)} %param.23) | copy-start | bytes 98308
  84.2 25.9 %copy-start.2 = (bf16[12,24,128]{2,1,0:T(8,128)(2,1)S(1)}, bf16[12,24,128]{2,1,0:T(8,128)(2,1)}, u32[]{:S(2)}) copy-start(bf16[12,24,128]{2,1,0:T(8,128)(2,1)} %all-reduce.3.cloned.1.call-done) | copy-start | bytes 221188
  84.2 26.4 %copy-start.3 = (bf16[128,512]{1,0:T(8,128)(2,1)S(1)}, bf16[128,512]{1,0:T(8,128)(2,1)}, u32[]{:S(2)}) copy-start(bf16[128,512]{1,0:T(8,128)(2,1)} %param.24) | copy-start | bytes 393220
Sparse Core Ops, SparseCore 0:
  44.8 19.3 all-reduce.2
  85.6 21.0 reduce-scatter.2
